TPU v7x, 32 devices: a whole 2x2x4 slice. The times are simulated.
32 devices in a mesh: row: 8 (over z, core), col: 4 (over y, x).
Axes of the slice: x: 2, y: 2, z: 4, core: 2. Of those that a mesh axis runs over, the one named last changes fastest.
Arguments:
- factor: float32 [10240, 10240], P('row', 'col'), may hold values from -1 to 6, as said below
Outputs:
- progressed: float32 [10240, 10240], P('row', 'col')
Inputs may be any that keep to these rules, and one draw needn't show every extreme that they name: factor is symmetric positive definite with smallest eigenvalue at least 0.5, stored in the block-cyclic order of the steps.
All inputs are finite; a program needn't handle non-finite values.
Results may differ from a plain program's by a relative error of at most 0.0001.
Values sent between devices are 32-bit elements; how exact they have to be, the bound alone decides.
A program may use at most 128 MiB of HBM per device.

v0:
```python
import jax
import jax.numpy as jnp
from jax import lax
from jax.sharding import PartitionSpec as P

TILE = 128
PIVOT = 512
STEPS = 2


def broadcast(value, axis, source):
    kept = jnp.where(lax.axis_index(axis) == source, value, 0).astype(value.dtype)
    return lax.psum(kept, axis)


def per_device(factor):
    rows_count = lax.axis_size("row")
    cols_count = lax.axis_size("col")
    local_rows, local_cols = factor.shape
    row_place = lax.axis_index("row")
    col_place = lax.axis_index("col")
    per_block = PIVOT // TILE
    row_offsets = jnp.arange(local_rows, dtype=jnp.int32)
    row_global = (row_offsets // TILE * rows_count + row_place) * TILE + row_offsets % TILE
    pivot_range = jnp.arange(PIVOT, dtype=jnp.int32)
    identity = jnp.eye(PIVOT, dtype=jnp.float32)

    def gather_columns(slab_of, step):
        slabs = []
        for member in range(per_block):
            tile_no = step * per_block + member
            slabs.append(broadcast(slab_of(tile_no), "col", tile_no % cols_count))
        return jnp.concatenate(slabs, axis=1)

    def plain_slab(matrix):

        def taker(tile_no):
            first = tile_no // cols_count * TILE
            return matrix[:, first : first + TILE]

        return taker

    matrix = factor
    column_panel = gather_columns(plain_slab(matrix), 0)
    for step in range(STEPS):
        row_parts = []
        block_parts = []
        for prepare_member in range(per_block):
            prepare_tile_no = step * per_block + prepare_member
            prepare_first = prepare_tile_no // rows_count * TILE
            got_rows, got_block = (
                broadcast(
                    matrix[prepare_first : prepare_first + TILE, :],
                    "row",
                    prepare_tile_no % rows_count,
                ),
                broadcast(
                    column_panel[prepare_first : prepare_first + TILE, :],
                    "row",
                    prepare_tile_no % rows_count,
                ),
            )
            row_parts.append(got_rows)
            block_parts.append(got_block)
        pivot_rows = jnp.concatenate(row_parts, axis=0)
        pivot_block = jnp.concatenate(block_parts, axis=0)
        lower = jnp.linalg.cholesky(pivot_block)
        prepare_inverse = jax.scipy.linalg.cho_solve((lower, True), identity)
        prepare_scaled = jnp.dot(
            prepare_inverse,
            pivot_rows,
            precision=lax.Precision.HIGHEST,
            preferred_element_type=jnp.float32,
        )
        prepare_marks = (row_global[:, None] - step * PIVOT == pivot_range[None, :]).astype(
            jnp.float32
        )
        prepare_reduced = column_panel - prepare_marks
        prepared = (prepare_inverse, prepare_scaled, prepare_marks, prepare_reduced)
        if step + 1 < STEPS:
            scaled_now = prepared[1]
            reduced_now = prepared[3]

            def early_slab(tile_no, source=matrix, scaled_now=scaled_now, reduced_now=reduced_now):
                first = tile_no // cols_count * TILE
                return source[:, first : first + TILE] - jnp.dot(
                    reduced_now,
                    scaled_now[:, first : first + TILE],
                    precision=lax.Precision.HIGHEST,
                    preferred_element_type=jnp.float32,
                )

            next_panel = gather_columns(early_slab, step + 1)
        inverse, scaled, marks, reduced = prepared
        updated = matrix - jnp.dot(
            reduced, scaled, precision=lax.Precision.HIGHEST, preferred_element_type=jnp.float32
        )
        fixed = marks - jnp.dot(
            reduced, inverse, precision=lax.Precision.HIGHEST, preferred_element_type=jnp.float32
        )
        for finish_member in range(per_block):
            finish_tile_no = step * per_block + finish_member
            finish_first = finish_tile_no // cols_count * TILE
            current = updated[:, finish_first : finish_first + TILE]
            chosen = jnp.where(
                col_place == finish_tile_no % cols_count,
                fixed[:, finish_member * TILE : (finish_member + 1) * TILE],
                current,
            )
            updated = updated.at[:, finish_first : finish_first + TILE].set(chosen)
        matrix = updated
        if step + 1 < STEPS:
            column_panel = next_panel
    return matrix


def solution(mesh):
    placed = (P("row", "col"),)
    return jax.shard_map(
        per_device, mesh=mesh, in_specs=placed, out_specs=P("row", "col"), check_vma=False
    )
```

profile of v0, /device:TPU:0, one launch (start us, length us, event | category | flops | bytes accessed | tf_op | source)
XLA Modules:
  0.0 923.6 jit_solution(14794230671533546266)
XLA Ops:
  6.5 13.9 %copy.5 = f32[1280,2560]{0,1:T(8,128)} copy(f32[1280,2560]{1,0:T(8,128)} %param.20) | data formatting | bytes 26214400 | tf_op args[0]
  23.1 3.8 slice_select_fusion.7
  26.9 77.3 %all-reduce.16.cloned.1.call-done = (f32[1280,128]{0,1:T(8,128)}, f32[1280,128]{0,1:T(8,128)}, f32[1280,128]{0,1:T(8,128)}, f32[1280,128]{0,1:T(8,128)}) async-done(((f32[1280,128]{0,1:T(8,128)}, f32[1280,128]{0,1:T(8,128)}, f32[1280,128]{0,1:T(8,128)}, f32[1280,128]{0,1:T(8,128)}), (f32[1280,128]{0,1:T(8,128)}, f32[1280,128]{0,1:T(8,128)}, f32[1280,128]{0,1:T(8,128)}, ...) | async-done | bytes 2621456 | tf_op jit(solution)/shard_map/psum | solution.py:13
  109.6 134.5 %all-reduce.12.cloned.1.call-done = (f32[128,2560]{0,1:T(8,128)}, f32[128,2560]{0,1:T(8,128)}, f32[128,2560]{0,1:T(8,128)}, f32[128,2560]{0,1:T(8,128)}, f32[128...) async-done(((f32[128,2560]{0,1:T(8,128)}, f32[128,2560]{0,1:T(8,128)}, f32[128,2560]{0,1:T(8,128)}, f32[128,2560]{0,1:T(8,128)}, ...) | async-done | bytes 6291472 | tf_op jit(solution)/shard_map/psum | solution.py:13
  256.2 11.7 %cholesky.286 = f32[128,128]{1,0:T(8,128)S(1)} custom-call(f32[128,128]{1,0:T(8,128)S(1)} %cholesky.426), custom_call_target="Cholesky" | custom-call | tf_op jit(solution)/shard_map/jit(cholesky)/cholesky | solution.py:67
  268.0 9.8 %custom-call.29 = f32[1,128,128]{1,2,0:T(8,128)S(1)} custom-call(f32[1,128,128]{2,1,0:T(8,128)S(1)} %get-tuple-element.214), custom_call_target="InvertDiagBlocksLowerTriangular" | custom-call | tf_op jit(solution)/shard_map/jit(cholesky)/cholesky | solution.py:67
  282.1 11.7 %cholesky.305 = f32[128,128]{1,0:T(8,128)S(1)} custom-call(f32[128,128]{1,0:T(8,128)S(1)} %cholesky.430), custom_call_target="Cholesky" | custom-call | tf_op jit(solution)/shard_map/jit(cholesky)/cholesky | solution.py:67
  294.5 10.0 %custom-call.30 = f32[1,128,128]{1,2,0:T(8,128)S(1)} custom-call(f32[1,128,128]{2,1,0:T(8,128)S(1)} %get-tuple-element.211), custom_call_target="InvertDiagBlocksLowerTriangular" | custom-call | tf_op jit(solution)/shard_map/jit(cholesky)/cholesky | solution.py:67
  306.9 11.7 %cholesky.326 = f32[128,128]{1,0:T(8,128)S(1)} custom-call(f32[128,128]{1,0:T(8,128)S(1)} %cholesky.435), custom_call_target="Cholesky" | custom-call | tf_op jit(solution)/shard_map/jit(cholesky)/cholesky | solution.py:67
  319.9 9.8 %custom-call.31 = f32[1,128,128]{1,2,0:T(8,128)S(1)} custom-call(f32[1,128,128]{2,1,0:T(8,128)S(1)} %get-tuple-element.208), custom_call_target="InvertDiagBlocksLowerTriangular" | custom-call | tf_op jit(solution)/shard_map/jit(cholesky)/cholesky | solution.py:67
  332.0 22.1 %cholesky.343 = f32[128,128]{1,0:T(8,128)S(1)} custom-call(f32[128,128]{1,0:T(8,128)S(1)} %convolution_subtract_fusion.20), custom_call_target="Cholesky" | custom-call | tf_op jit(solution)/shard_map/jit(cholesky)/cholesky | solution.py:67
  360.9 11.7 %while.12 = (s32[]{:T(128)}, f32[512,512]{1,0:T(8,128)}, s32[4,2]{0,1:T(2,128)S(1)}, f32[4,128,128]{2,1,0:T(8,128)S(1)}, s32[]{:T(128)}) while((s32[]{:T(128)}, f32[512,512]{1,0:T(8,128)}, s32[4,2]{0,1:T(2,128)S(1)}, f32[4,128,128]{2,1,0:T(8,128)S(1)}, s32[]{:T(128)}) %tuple.105), condition=%wide.while_cond.8, body=%wide.while_body.8.sunk | while | flops 2 | bytes 131189 | solution.py:68
  372.6 39.3 %custom-call.32 = f32[4,128,128]{1,2,0:T(8,128)S(1)} custom-call(f32[4,128,128]{2,1,0:T(8,128)S(1)} %get-tuple-element.117), custom_call_target="InvertDiagBlocksLowerTriangular" | custom-call | tf_op jit(solution)/shard_map/jit(_cho_solve)/triangular_solve | solution.py:68
  422.3 6.2 convert_subtract_fusion.2
  428.6 9.2 fusion
  441.5 26.3 %convolution_subtract_fusion.1 = f32[1280,2560]{0,1:T(8,128)} fusion(f32[1280,2560]{0,1:T(8,128)S(1)} %bitcast.117, f32[512,2560]{1,0:T(8,128)S(1)} %fusion, f32[1280,512]{0,1:T(8,128)S(1)} %constant_dynamic-update-slice_fusion, s32[1280]{0:T(1024)S(1)} %fusion.122), kind=kOutput, calls=%fused_computation.5 | convolution fusion | flops 20137902080 | bytes 34083840 | tf_op jit(solution)/shard_map/dot_general | solution.py:95
  476.6 3.8 slice_select_fusion.3
  480.3 65.9 %all-reduce.14.cloned.1.call-done = (f32[1280,128]{0,1:T(8,128)}, f32[1280,128]{0,1:T(8,128)}, f32[1280,128]{0,1:T(8,128)}, f32[1280,128]{0,1:T(8,128)}) async-done(((f32[1280,128]{0,1:T(8,128)}, f32[1280,128]{0,1:T(8,128)}, f32[1280,128]{0,1:T(8,128)}, f32[1280,128]{0,1:T(8,128)}), (f32[1280,128]{0,1:T(8,128)}, f32[1280,128]{0,1:T(8,128)}, f32[1280,128]{0,1:T(8,128)}, ...) | async-done | bytes 2621456 | tf_op jit(solution)/shard_map/psum | solution.py:13
  550.8 135.4 %all-reduce.10.cloned.1.call-done = (f32[128,2560]{0,1:T(8,128)}, f32[128,2560]{0,1:T(8,128)}, f32[128,2560]{0,1:T(8,128)}, f32[128,2560]{0,1:T(8,128)}, f32[128...) async-done(((f32[128,2560]{0,1:T(8,128)}, f32[128,2560]{0,1:T(8,128)}, f32[128,2560]{0,1:T(8,128)}, f32[128,2560]{0,1:T(8,128)}, ...) | async-done | bytes 6291472 | tf_op jit(solution)/shard_map/psum | solution.py:13
  698.4 11.7 %cholesky.358 = f32[128,128]{1,0:T(8,128)S(1)} custom-call(f32[128,128]{1,0:T(8,128)S(1)} %cholesky.439), custom_call_target="Cholesky" | custom-call | tf_op jit(solution)/shard_map/jit(cholesky)/cholesky | solution.py:67
  710.8 9.8 %custom-call.33 = f32[1,128,128]{1,2,0:T(8,128)S(1)} custom-call(f32[1,128,128]{2,1,0:T(8,128)S(1)} %get-tuple-element.204), custom_call_target="InvertDiagBlocksLowerTriangular" | custom-call | tf_op jit(solution)/shard_map/jit(cholesky)/cholesky | solution.py:67
  724.9 11.7 %cholesky.377 = f32[128,128]{1,0:T(8,128)S(1)} custom-call(f32[128,128]{1,0:T(8,128)S(1)} %cholesky.443), custom_call_target="Cholesky" | custom-call | tf_op jit(solution)/shard_map/jit(cholesky)/cholesky | solution.py:67
  738.0 10.2 %custom-call.34 = f32[1,128,128]{1,2,0:T(8,128)S(1)} custom-call(f32[1,128,128]{2,1,0:T(8,128)S(1)} %get-tuple-element.201), custom_call_target="InvertDiagBlocksLowerTriangular" | custom-call | tf_op jit(solution)/shard_map/jit(cholesky)/cholesky | solution.py:67
  750.5 11.7 %cholesky.398 = f32[128,128]{1,0:T(8,128)S(1)} custom-call(f32[128,128]{1,0:T(8,128)S(1)} %cholesky.448), custom_call_target="Cholesky" | custom-call | tf_op jit(solution)/shard_map/jit(cholesky)/cholesky | solution.py:67
  763.5 9.8 %custom-call.35 = f32[1,128,128]{1,2,0:T(8,128)S(1)} custom-call(f32[1,128,128]{2,1,0:T(8,128)S(1)} %get-tuple-element.198), custom_call_target="InvertDiagBlocksLowerTriangular" | custom-call | tf_op jit(solution)/shard_map/jit(cholesky)/cholesky | solution.py:67
  775.6 11.9 %cholesky.415 = f32[128,128]{1,0:T(8,128)S(1)} custom-call(f32[128,128]{1,0:T(8,128)S(1)} %convolution_subtract_fusion.19), custom_call_target="Cholesky" | custom-call | tf_op jit(solution)/shard_map/jit(cholesky)/cholesky | solution.py:67
  793.5 11.7 %while.13 = (s32[]{:T(128)}, f32[512,512]{1,0:T(8,128)}, s32[4,2]{0,1:T(2,128)S(1)}, f32[4,128,128]{2,1,0:T(8,128)S(1)}, s32[]{:T(128)}) while((s32[]{:T(128)}, f32[512,512]{1,0:T(8,128)}, s32[4,2]{0,1:T(2,128)S(1)}, f32[4,128,128]{2,1,0:T(8,128)S(1)}, s32[]{:T(128)}) %tuple.123), condition=%wide.while_cond.8.clone, body=%wide.while_body.8.clone.sunk | while | flops 2 | bytes 131189 | solution.py:68
  805.2 39.3 %custom-call.36 = f32[4,128,128]{1,2,0:T(8,128)S(1)} custom-call(f32[4,128,128]{2,1,0:T(8,128)S(1)} %get-tuple-element.118), custom_call_target="InvertDiagBlocksLowerTriangular" | custom-call | tf_op jit(solution)/shard_map/jit(_cho_solve)/triangular_solve | solution.py:68
  854.9 5.0 convert_subtract_fusion
  860.0 9.2 fusion.8
  869.3 25.8 %convolution_subtract_fusion = f32[1280,2560]{0,1:T(8,128)} fusion(f32[1280,2560]{0,1:T(8,128)S(1)} %bitcast.119, f32[512,2560]{1,0:T(8,128)S(1)} %fusion.8, f32[1280,512]{0,1:T(8,128)S(1)} %constant_dynamic-update-slice_fusion.8, s32[1280]{0:T(1024)S(1)} %broadcast_add_fusion), kind=kOutput, calls=%fused_computation.4 | convolution fusion | flops 20137902080 | bytes 34083840 | tf_op jit(solution)/shard_map/dot_general | solution.py:95
  902.8 13.9 %copy.13 = f32[1280,2560]{1,0:T(8,128)} copy(f32[1280,2560]{0,1:T(8,128)} %fusion.45) | data formatting | bytes 26214400 | tf_op jit(solution)/shard_map/scatter | solution.py:110
  (190 shorter events, 131.9 us)
Async XLA Ops:
  6.5 97.7 %all-reduce.16.cloned.1.call-start = ((), (), s32[]{:S(2)}) async-start(), calls=%async_computation.3 | async-start | bytes 5242880 | tf_op jit(solution)/shard_map/psum | solution.py:13
  23.1 221.0 %all-reduce.12.cloned.1.call-start = ((), (), s32[]{:S(2)}) async-start(), calls=%async_computation.1 | async-start | bytes 12582912 | tf_op jit(solution)/shard_map/psum | solution.py:13
  104.2 2.4 copy-start.8
  104.2 2.4 copy-start.7
  107.8 438.5 %all-reduce.14.cloned.1.call-start = ((), (), s32[]{:S(2)}) async-start(), calls=%async_computation.2 | async-start | bytes 5242880 | tf_op jit(solution)/shard_map/psum | solution.py:13
  255.2 1.0 copy-start.4
  411.9 5.3 copy-start.2
  415.1 22.6 %slice-start = ((s8[13107200]{0:T(1024)(128)(4,1)}), s8[4194304]{0:T(1024)(128)(4,1)S(1)}, s32[]{:S(2)}) async-start(s8[13107200]{0:T(1024)(128)(4,1)} %bitcast.116), calls=%async_computation.4 | async-start | bytes 8388608
  420.4 8.2 copy-start.12
  420.9 16.9 %slice-start.1 = ((s8[13107200]{0:T(1024)(128)(4,1)}), s8[4194304]{0:T(1024)(128)(4,1)S(1)}, s32[]{:S(2)}) async-start(s8[13107200]{0:T(1024)(128)(4,1)} %bitcast.116), calls=%async_computation.5 | async-start | bytes 8388608
  421.9 6.7 copy-start.9
  421.9 6.7 copy-start.10
  421.9 6.6 copy-start.11
  422.3 15.5 %slice-start.2 = ((s8[13107200]{0:T(1024)(128)(4,1)}), s8[4194304]{0:T(1024)(128)(4,1)S(1)}, s32[]{:S(2)}) async-start(s8[13107200]{0:T(1024)(128)(4,1)} %bitcast.116), calls=%async_computation.6 | async-start | bytes 8388608
  428.6 9.2 slice-start.3
  467.7 1.7 copy-start
  467.7 218.4 %all-reduce.10.cloned.1.call-start = ((), (), s32[]{:S(2)}) async-start(), calls=%async_computation | async-start | bytes 12582912 | tf_op jit(solution)/shard_map/psum | solution.py:13
  546.3 2.4 copy-start.6
  546.3 2.4 copy-start.5
  697.4 1.0 copy-start.3
  844.5 5.3 copy-start.1
  847.8 21.4 %slice-start.4 = ((s8[13107200]{0:T(1024)(128)(4,1)}), s8[4194304]{0:T(1024)(128)(4,1)S(1)}, s32[]{:S(2)}) async-start(s8[13107200]{0:T(1024)(128)(4,1)} %bitcast.118), calls=%async_computation.8 | async-start | bytes 8388608
  853.0 7.0 copy-start.16
  853.5 15.7 %slice-start.5 = ((s8[13107200]{0:T(1024)(128)(4,1)}), s8[4194304]{0:T(1024)(128)(4,1)S(1)}, s32[]{:S(2)}) async-start(s8[13107200]{0:T(1024)(128)(4,1)} %bitcast.118), calls=%async_computation.9 | async-start | bytes 8388608
  854.5 5.4 copy-start.13
  854.5 5.4 copy-start.14
  854.5 5.4 copy-start.15
  854.9 14.3 %slice-start.6 = ((s8[13107200]{0:T(1024)(128)(4,1)}), s8[4194304]{0:T(1024)(128)(4,1)S(1)}, s32[]{:S(2)}) async-start(s8[13107200]{0:T(1024)(128)(4,1)} %bitcast.118), calls=%async_computation.10 | async-start | bytes 8388608
  860.0 9.2 %slice-start.7 = ((s8[13107200]{0:T(1024)(128)(4,1)}), s8[524288]{0:T(1024)(128)(4,1)S(1)}, s32[]{:S(2)}) async-start(s8[13107200]{0:T(1024)(128)(4,1)} %bitcast.118), calls=%async_computation.11 | async-start | bytes 1048576
Sparse Core Ops, SparseCore 0:
  23.2 80.9 all-reduce.15
  107.9 136.1 all-reduce.11
  467.9 78.3 all-reduce.13
  550.0 136.1 all-reduce.9
where the time goes:
time: 935 us; the launch traced here: 924 us
  waiting for transfers between devices  413 us (44%)
  other arithmetic  289 us (31%)
  matrix products  121 us (13%)
  local copies, waits for them, and re-layouts  80.7 us (9%)
  between operations  19.2 us (2%)
    psum x4, waiting for transfers between devices, broadcast(): return lax.psum(kept, axis)  413 us
    another operation x29, other arithmetic, per_device(): lower = jnp.linalg.cholesky(pivot_block)  172 us
    another operation x5, other arithmetic, per_device(): prepare_inverse = jax.scipy.linalg.cho_solve((lower, True), identity)  83.3 us
    dot_general x2, matrix products, per_device(): jnp.dot(reduced, scaled, precision=lax.Precision.HIGHEST, preferred_eleme...  52.1 us
    unnamed x63, local copies, waits for them, and re-layouts  32.7 us
    another operation x27, local copies, waits for them, and re-layouts, per_device(): prepare_inverse = jax.scipy.linalg.cho_solve((lower, True), identity)  23.3 us
    another operation x28, matrix products, per_device(): prepare_inverse = jax.scipy.linalg.cho_solve((lower, True), identity)  20.5 us
  transfers between devices with their start and end apart: 4, of which 4 were waited for; matrix products, arithmetic and copies ran while one was open for 2% of the time, Pallas kernels for 0%

commit v1 on v0

--- a/solution.py
+++ b/solution.py
@@ -10,7 +10,8 @@
 
 def broadcast(value, axis, source):
     kept = jnp.where(lax.axis_index(axis) == source, value, 0).astype(value.dtype)
-    return lax.psum(kept, axis)
+    connect_stages_all = lambda shard_axis, q_in: lax.all_gather(q_in, shard_axis).sum(axis=0)
+    return connect_stages_all(axis, kept)
 
 
 def per_device(factor):

time: 935 us -> 1470 us (1.57)
  waiting for transfers between devices: 413 us -> 924 us
  other arithmetic: 289 us -> 356 us
  local copies, waits for them, and re-layouts: 80.7 us -> 42.2 us
    all_gather x0 -> x24, waiting for transfers between devices: none -> 914 us  [broadcast(): lax.all_gather(q_in, shard_axis).sum(axis=0)]
    psum x4 -> x0, waiting for transfers between devices: 413 us -> none  [broadcast(): return lax.psum(kept, axis)]
    reduce_sum x0 -> x24, other arithmetic: none -> 83.7 us  [broadcast(): lax.all_gather(q_in, shard_axis).sum(axis=0)]
    unnamed x63 -> x64, local copies, waits for them, and re-layouts: 32.7 us -> 13.7 us
  transfers between devices with their start and end apart: 4 -> 24, of which waited for: 4 -> 21; matrix products, arithmetic and copies ran while one was open for 2% -> 29% of each run, Pallas kernels for 0% -> 0%
where the time goes in v1:
time: 1470 us; the launch traced here: 1460 us
  waiting for transfers between devices  924 us (63%)
  other arithmetic  356 us (24%)
  matrix products  121 us (8%)
  local copies, waits for them, and re-layouts  42.2 us (3%)
  between operations  20.2 us (1%)
    all_gather x24, waiting for transfers between devices, broadcast(): lax.all_gather(q_in, shard_axis).sum(axis=0)  914 us
    another operation x29, other arithmetic, per_device(): lower = jnp.linalg.cholesky(pivot_block)  164 us
    reduce_sum x24, other arithmetic, broadcast(): lax.all_gather(q_in, shard_axis).sum(axis=0)  83.7 us
    another operation x5, other arithmetic, per_device(): prepare_inverse = jax.scipy.linalg.cho_solve((lower, True), identity)  81.9 us
    dot_general x2, matrix products, per_device(): jnp.dot(reduced, scaled, precision=lax.Precision.HIGHEST, preferred_eleme...  51.8 us
  transfers between devices with their start and end apart: 24, of which 21 were waited for; matrix products, arithmetic and copies ran while one was open for 29% of the time, Pallas kernels for 0%

profile of v1, /device:TPU:0, one launch (start us, length us, event | category | flops | bytes accessed | tf_op | source)
XLA Modules:
  0.0 1464.3 jit_solution(11056793224778936984)
XLA Ops:
  11.3 40.3 %all-gather.49.cloned.1.call-done = f32[5120,128]{1,0:T(8,128)} async-done(((f32[1280,128]{1,0:T(8,128)}), f32[5120,128]{1,0:T(8,128)}) %all-gather.49.cloned.1.call-update) | async-done | bytes 2621456 | tf_op jit(solution)/shard_map/all_gather | solution.py:13
  53.5 39.4 %all-gather.51.cloned.1.call-done = f32[5120,128]{1,0:T(8,128)} async-done(((f32[1280,128]{1,0:T(8,128)}), f32[5120,128]{1,0:T(8,128)}) %all-gather.51.cloned.1.call-update) | async-done | bytes 2621456 | tf_op jit(solution)/shard_map/all_gather | solution.py:13
  94.9 39.4 %all-gather.53.cloned.1.call-done = f32[5120,128]{1,0:T(8,128)} async-done(((f32[1280,128]{1,0:T(8,128)}), f32[5120,128]{1,0:T(8,128)}) %all-gather.53.cloned.1.call-update) | async-done | bytes 2621456 | tf_op jit(solution)/shard_map/all_gather | solution.py:13
  136.3 39.3 %all-gather.55.cloned.1.call-done = f32[5120,128]{1,0:T(8,128)} async-done(((f32[1280,128]{1,0:T(8,128)}), f32[5120,128]{1,0:T(8,128)}) %all-gather.55.cloned.1.call-update) | async-done | bytes 2621456 | tf_op jit(solution)/shard_map/all_gather | solution.py:13
  187.5 20.6 %all-gather.57.cloned.1.call-done = f32[1024,512]{1,0:T(8,128)} async-done(((f32[128,512]{1,0:T(8,128)}), f32[1024,512]{1,0:T(8,128)}) %all-gather.57.cloned.1.call-update) | async-done | bytes 2097168 | tf_op jit(solution)/shard_map/all_gather | solution.py:13
  210.0 28.1 %all-gather.59.cloned.1.call-done = f32[1024,512]{1,0:T(8,128)} async-done(((f32[128,512]{1,0:T(8,128)}), f32[1024,512]{1,0:T(8,128)}) %all-gather.59.cloned.1.call-update) | async-done | bytes 2097168 | tf_op jit(solution)/shard_map/all_gather | solution.py:13
  240.1 28.2 %all-gather.61.cloned.1.call-done = f32[1024,512]{1,0:T(8,128)} async-done(((f32[128,512]{1,0:T(8,128)}), f32[1024,512]{1,0:T(8,128)}) %all-gather.61.cloned.1.call-update) | async-done | bytes 2097168 | tf_op jit(solution)/shard_map/all_gather | solution.py:13
  270.2 28.2 %all-gather.63.cloned.1.call-done = f32[1024,512]{1,0:T(8,128)} async-done(((f32[128,512]{1,0:T(8,128)}), f32[1024,512]{1,0:T(8,128)}) %all-gather.63.cloned.1.call-update) | async-done | bytes 2097168 | tf_op jit(solution)/shard_map/all_gather | solution.py:13
  307.9 11.7 cholesky.286
  332.7 12.1 cholesky.305
  357.8 13.2 cholesky.326
  386.5 11.9 cholesky.343
  406.3 14.4 while.12
  420.7 40.8 %custom-call.32 = f32[4,128,128]{1,2,0:T(8,128)} custom-call(f32[4,128,128]{2,1,0:T(8,128)} %get-tuple-element.117), custom_call_target="InvertDiagBlocksLowerTriangular" | custom-call | tf_op jit(solution)/shard_map/jit(_cho_solve)/triangular_solve | solution.py:69
  478.1 20.0 %all-gather.67.cloned.1.call-done = f32[1024,2560]{1,0:T(8,128)} async-done(((f32[128,2560]{1,0:T(8,128)}), f32[1024,2560]{1,0:T(8,128)}) %all-gather.67.cloned.1.call-update) | async-done | bytes 10485776 | tf_op jit(solution)/shard_map/all_gather | solution.py:13
  504.3 93.2 %all-gather.69.cloned.1.call-done = f32[1024,2560]{1,0:T(8,128)} async-done(((f32[128,2560]{1,0:T(8,128)}), f32[1024,2560]{1,0:T(8,128)}) %all-gather.69.cloned.1.call-update) | async-done | bytes 10485776 | tf_op jit(solution)/shard_map/all_gather | solution.py:13
  603.7 93.1 %all-gather.71.cloned.1.call-done = f32[1024,2560]{1,0:T(8,128)} async-done(((f32[128,2560]{1,0:T(8,128)}), f32[1024,2560]{1,0:T(8,128)}) %all-gather.71.cloned.1.call-update) | async-done | bytes 10485776 | tf_op jit(solution)/shard_map/all_gather | solution.py:13
  721.1 36.2 %all-gather.73.cloned.1.call-done = f32[5120,128]{1,0:T(8,128)} async-done(((f32[1280,128]{1,0:T(8,128)}), f32[5120,128]{1,0:T(8,128)}) %all-gather.73.cloned.1.call-update) | async-done | bytes 2621456 | tf_op jit(solution)/shard_map/all_gather | solution.py:13
  760.1 38.4 %all-gather.75.cloned.1.call-done = f32[5120,128]{1,0:T(8,128)} async-done(((f32[1280,128]{1,0:T(8,128)}), f32[5120,128]{1,0:T(8,128)}) %all-gather.75.cloned.1.call-update) | async-done | bytes 2621456 | tf_op jit(solution)/shard_map/all_gather | solution.py:13
  801.3 38.5 %all-gather.77.cloned.1.call-done = f32[5120,128]{1,0:T(8,128)} async-done(((f32[1280,128]{1,0:T(8,128)}), f32[5120,128]{1,0:T(8,128)}) %all-gather.77.cloned.1.call-update) | async-done | bytes 2621456 | tf_op jit(solution)/shard_map/all_gather | solution.py:13
  842.6 38.4 %all-gather.79.cloned.1.call-done = f32[5120,128]{1,0:T(8,128)} async-done(((f32[1280,128]{1,0:T(8,128)}), f32[5120,128]{1,0:T(8,128)}) %all-gather.79.cloned.1.call-update) | async-done | bytes 2621456 | tf_op jit(solution)/shard_map/all_gather | solution.py:13
  896.2 26.0 %convolution_subtract_fusion.1 = f32[1280,2560]{1,0:T(8,128)S(1)} fusion(f32[1280,2560]{1,0:T(8,128)} %param.20, f32[512,2560]{1,0:T(8,128)} %copy-done.10, s32[1280]{0:T(1024)S(1)} %fusion.122, f32[1280,128]{1,0:T(8,128)} %copy-done.4, f32[1280,128]{1,0:T(8,128)S(1)} %copy-done.3, f32[1280,128]{1,0:T(8,128)S(1)} %reduce_sum.217, ...), kind=kOutput, calls=%fused_computation.5 | convolution fusion | flops 20139868160 | bytes 34083840 | tf_op jit(solution)/shard_map/dot_general | solution.py:96
  948.1 28.2 %all-gather.87.cloned.1.call-done = f32[1024,512]{1,0:T(8,128)} async-done(((f32[128,512]{1,0:T(8,128)}), f32[1024,512]{1,0:T(8,128)}) %all-gather.87.cloned.1.call-update) | async-done | bytes 2097168 | tf_op jit(solution)/shard_map/all_gather | solution.py:13
  978.2 28.1 %all-gather.81.cloned.1.call-done = f32[1024,512]{1,0:T(8,128)} async-done(((f32[128,512]{1,0:T(8,128)}), f32[1024,512]{1,0:T(8,128)}) %all-gather.81.cloned.1.call-update) | async-done | bytes 2097168 | tf_op jit(solution)/shard_map/all_gather | solution.py:13
  1010.7 11.7 cholesky.358
  1033.0 12.1 cholesky.377
  1077.8 11.9 cholesky.415
  1103.3 39.3 %custom-call.36 = f32[4,128,128]{1,2,0:T(8,128)S(1)} custom-call(f32[4,128,128]{2,1,0:T(8,128)S(1)} %get-tuple-element.118), custom_call_target="InvertDiagBlocksLowerTriangular" | custom-call | tf_op jit(solution)/shard_map/jit(_cho_solve)/triangular_solve | solution.py:69
  1164.8 41.9 %all-gather.91.cloned.1.call-done = f32[1024,2560]{1,0:T(8,128)} async-done(((f32[128,2560]{1,0:T(8,128)}), f32[1024,2560]{1,0:T(8,128)}) %all-gather.91.cloned.1.call-update) | async-done | bytes 10485776 | tf_op jit(solution)/shard_map/all_gather | solution.py:13
  1212.9 93.2 %all-gather.93.cloned.1.call-done = f32[1024,2560]{1,0:T(8,128)} async-done(((f32[128,2560]{1,0:T(8,128)}), f32[1024,2560]{1,0:T(8,128)}) %all-gather.93.cloned.1.call-update) | async-done | bytes 10485776 | tf_op jit(solution)/shard_map/all_gather | solution.py:13
  1312.4 92.9 %all-gather.95.cloned.1.call-done = f32[1024,2560]{1,0:T(8,128)} async-done(((f32[128,2560]{1,0:T(8,128)}), f32[1024,2560]{1,0:T(8,128)}) %all-gather.95.cloned.1.call-update) | async-done | bytes 10485776 | tf_op jit(solution)/shard_map/all_gather | solution.py:13
  1422.3 25.8 %convolution_subtract_fusion = f32[1280,2560]{1,0:T(8,128)S(1)} fusion(f32[1280,2560]{1,0:T(8,128)} %copy-done, f32[512,2560]{1,0:T(8,128)S(1)} %fusion.8, s32[1280]{0:T(1024)S(1)} %broadcast_add_fusion, f32[1280,128]{1,0:T(8,128)S(1)} %copy-done.9, f32[1280,128]{1,0:T(8,128)S(1)} %copy-done.8, f32[1280,128]{1,0:T(8,128)S(1)} %copy-done.7, ...), kind=kOutput, calls=%fused_computation.4 | convolution fusion | flops 20139868160 | bytes 34083840 | tf_op jit(solution)/shard_map/dot_general | solution.py:96
  (280 shorter events, 330.2 us)
Async XLA Ops:
  6.5 45.0 %all-gather.49.cloned.1.call-start = ((), (), s32[]{:S(2)}) async-start(), calls=%async_computation | async-start | bytes 3276800 | tf_op jit(solution)/shard_map/all_gather | solution.py:13
  9.2 83.8 %all-gather.51.cloned.1.call-start = ((), (), s32[]{:S(2)}) async-start(), calls=%async_computation.1 | async-start | bytes 3276800 | tf_op jit(solution)/shard_map/all_gather | solution.py:13
  9.9 124.4 %all-gather.53.cloned.1.call-start = ((), (), s32[]{:S(2)}) async-start(), calls=%async_computation.2 | async-start | bytes 3276800 | tf_op jit(solution)/shard_map/all_gather | solution.py:13
  10.7 164.9 %all-gather.55.cloned.1.call-start = ((), (), s32[]{:S(2)}) async-start(), calls=%async_computation.3 | async-start | bytes 3276800 | tf_op jit(solution)/shard_map/all_gather | solution.py:13
  11.2 196.8 %all-gather.57.cloned.1.call-start = ((), (), s32[]{:S(2)}) async-start(), calls=%async_computation.4 | async-start | bytes 2359296 | tf_op jit(solution)/shard_map/all_gather | solution.py:13
  136.3 41.4 %copy-start.2 = (f32[1280,128]{1,0:T(8,128)}, f32[1280,128]{1,0:T(8,128)S(1)}, u32[]{:S(2)}) copy-start(f32[1280,128]{1,0:T(8,128)S(1)} %reduce_sum.218) | copy-start | bytes 1966084
  178.8 59.3 %all-gather.59.cloned.1.call-start = ((), (), s32[]{:S(2)}) async-start(), calls=%async_computation.5 | async-start | bytes 2359296 | tf_op jit(solution)/shard_map/all_gather | solution.py:13
  179.3 88.9 %all-gather.61.cloned.1.call-start = ((), (), s32[]{:S(2)}) async-start(), calls=%async_computation.6 | async-start | bytes 2359296 | tf_op jit(solution)/shard_map/all_gather | solution.py:13
  180.1 118.4 %all-gather.63.cloned.1.call-start = ((), (), s32[]{:S(2)}) async-start(), calls=%async_computation.7 | async-start | bytes 2359296 | tf_op jit(solution)/shard_map/all_gather | solution.py:13
  180.8 291.2 %all-gather.65.cloned.1.call-start = ((), (), s32[]{:S(2)}) async-start(), calls=%async_computation.8 | async-start | bytes 11796480 | tf_op jit(solution)/shard_map/all_gather | solution.py:13
  184.7 313.4 %all-gather.67.cloned.1.call-start = ((), (), s32[]{:S(2)}) async-start(), calls=%async_computation.9 | async-start | bytes 11796480 | tf_op jit(solution)/shard_map/all_gather | solution.py:13
  185.3 412.2 %all-gather.69.cloned.1.call-start = ((), (), s32[]{:S(2)}) async-start(), calls=%async_computation.10 | async-start | bytes 11796480 | tf_op jit(solution)/shard_map/all_gather | solution.py:13
  186.1 510.7 %all-gather.71.cloned.1.call-start = ((), (), s32[]{:S(2)}) async-start(), calls=%async_computation.11 | async-start | bytes 11796480 | tf_op jit(solution)/shard_map/all_gather | solution.py:13
  186.6 570.7 %all-gather.73.cloned.1.call-start = ((), (), s32[]{:S(2)}) async-start(), calls=%async_computation.12 | async-start | bytes 3276800 | tf_op jit(solution)/shard_map/all_gather | solution.py:13
  210.0 92.1 %copy-start.19 = (f32[128,512]{0,1:T(8,128)}, f32[128,512]{0,1:T(8,128)S(1)}, u32[]{:S(2)}) copy-start(f32[128,512]{0,1:T(8,128)S(1)} %copy.4) | copy-start | bytes 786436
  240.1 62.0 %copy-start.20 = (f32[128,512]{0,1:T(8,128)}, f32[128,512]{0,1:T(8,128)S(1)}, u32[]{:S(2)}) copy-start(f32[128,512]{0,1:T(8,128)S(1)} %copy.5) | copy-start | bytes 786436
  270.2 31.9 %copy-start.22 = (f32[128,512]{0,1:T(8,128)}, f32[128,512]{0,1:T(8,128)S(1)}, u32[]{:S(2)}) copy-start(f32[128,512]{0,1:T(8,128)S(1)} %copy.6) | copy-start | bytes 786436
  420.7 46.4 %copy-start.12 = (f32[512,512]{1,0:T(8,128)S(1)}, f32[512,512]{1,0:T(8,128)}, u32[]{:S(2)}) copy-start(f32[512,512]{1,0:T(8,128)} %get-tuple-element.334) | copy-start | bytes 3145732
  719.3 79.2 %all-gather.75.cloned.1.call-start = ((), (), s32[]{:S(2)}) async-start(), calls=%async_computation.13 | async-start | bytes 3276800 | tf_op jit(solution)/shard_map/all_gather | solution.py:13
  719.9 119.9 %all-gather.77.cloned.1.call-start = ((), (), s32[]{:S(2)}) async-start(), calls=%async_computation.14 | async-start | bytes 3276800 | tf_op jit(solution)/shard_map/all_gather | solution.py:13
  720.5 160.5 %all-gather.79.cloned.1.call-start = ((), (), s32[]{:S(2)}) async-start(), calls=%async_computation.15 | async-start | bytes 3276800 | tf_op jit(solution)/shard_map/all_gather | solution.py:13
  721.1 214.9 %all-gather.83.cloned.1.call-start = ((), (), s32[]{:S(2)}) async-start(), calls=%async_computation.17 | async-start | bytes 2359296 | tf_op jit(solution)/shard_map/all_gather | solution.py:13
  886.7 59.4 %all-gather.85.cloned.1.call-start = ((), (), s32[]{:S(2)}) async-start(), calls=%async_computation.18 | async-start | bytes 2359296 | tf_op jit(solution)/shard_map/all_gather | solution.py:13
  887.3 89.0 %all-gather.87.cloned.1.call-start = ((), (), s32[]{:S(2)}) async-start(), calls=%async_computation.19 | async-start | bytes 2359296 | tf_op jit(solution)/shard_map/all_gather | solution.py:13
  888.1 118.2 %all-gather.81.cloned.1.call-start = ((), (), s32[]{:S(2)}) async-start(), calls=%async_computation.16 | async-start | bytes 2359296 | tf_op jit(solution)/shard_map/all_gather | solution.py:13
  896.2 262.5 %all-gather.89.cloned.1.call-start = ((), (), s32[]{:S(2)}) async-start(), calls=%async_computation.20 | async-start | bytes 11796480 | tf_op jit(solution)/shard_map/all_gather | solution.py:13
  933.0 273.8 %all-gather.91.cloned.1.call-start = ((), (), s32[]{:S(2)}) async-start(), calls=%async_computation.21 | async-start | bytes 11796480 | tf_op jit(solution)/shard_map/all_gather | solution.py:13
  933.7 372.3 %all-gather.93.cloned.1.call-start = ((), (), s32[]{:S(2)}) async-start(), calls=%async_computation.22 | async-start | bytes 11796480 | tf_op jit(solution)/shard_map/all_gather | solution.py:13
  934.5 470.8 %all-gather.95.cloned.1.call-start = ((), (), s32[]{:S(2)}) async-start(), calls=%async_computation.23 | async-start | bytes 11796480 | tf_op jit(solution)/shard_map/all_gather | solution.py:13
  948.1 60.2 %copy-start.21 = (f32[128,512]{0,1:T(8,128)}, f32[128,512]{0,1:T(8,128)S(1)}, u32[]{:S(2)}) copy-start(f32[128,512]{0,1:T(8,128)S(1)} %copy.11) | copy-start | bytes 786436
  978.2 30.0 %copy-start.23 = (f32[128,512]{0,1:T(8,128)}, f32[128,512]{0,1:T(8,128)S(1)}, u32[]{:S(2)}) copy-start(f32[128,512]{0,1:T(8,128)S(1)} %copy.12) | copy-start | bytes 786436
  1103.3 42.1 %copy-start.11 = (f32[512,512]{1,0:T(8,128)}, f32[512,512]{1,0:T(8,128)S(1)}, u32[]{:S(2)}) copy-start(f32[512,512]{1,0:T(8,128)S(1)} %get-tuple-element.333) | copy-start | bytes 3145732
  (24 other events, 144.0 us)
Sparse Core Ops, SparseCore 0:
  9.3 42.2 all-gather.48
  53.4 39.4 all-gather.50
  94.8 39.4 all-gather.52
  136.0 39.4 all-gather.54
  178.9 29.1 all-gather.56
  209.5 28.5 all-gather.58
  239.7 28.5 all-gather.60
  269.9 28.5 all-gather.62
  300.1 98.8 all-gather.64
  400.4 97.6 all-gather.66
  499.8 97.6 all-gather.68
  599.0 97.6 all-gather.70
  719.5 37.8 all-gather.72
  759.0 39.4 all-gather.74
  800.3 39.4 all-gather.76
  841.5 39.4 all-gather.78
  886.9 29.1 all-gather.82
  917.5 28.5 all-gather.84
  947.7 28.5 all-gather.86
  977.7 28.5 all-gather.80
  1008.0 98.9 all-gather.88
  1108.5 98.1 all-gather.90
  1208.4 97.6 all-gather.92
  1307.6 97.6 all-gather.94
